TPU v7x, 32 devices: a whole 2x2x4 slice. The times are simulated.
32 devices in a mesh: batch: 4 (over y, core), proto: 8 (over z, x).
Axes of the slice: x: 2, y: 2, z: 4, core: 2. Of those that a mesh axis runs over, the one named last changes fastest.
Arguments:
- features: bfloat16 [4096, 256], P(('batch', 'proto')), may hold values from -8 to 8
- head_weight: bfloat16 [256, 65536], P('batch', 'proto'), may hold values from -0.375 to 0.375
- student_scores: bfloat16 [2, 4096, 65536], P(None, 'batch', 'proto'), may hold values from -1 to 1
Outputs:
- targets: bfloat16 [4096, 65536], P('batch', 'proto')
- row_loss: float32 [2, 4096], P(None, 'batch')
All inputs are finite; a program needn't handle non-finite values.
Results may differ from a plain program's by a relative error of at most 0.0013.
Values may be sent and summed in bfloat16 or wider, within the bound.
No kernel may reach another device: no remote copies, remote signals or barrier semaphores. Data moves between devices by JAX's collectives and lax.ppermute only.
A program may use at most 192 MiB of HBM per device.

v0:
```python
import jax
import jax.numpy as jnp
from jax import lax
from jax.sharding import PartitionSpec as P

PROTOS = 65536
ITERS = 3
TEACHER_TEMP = 0.07
STUDENT_TEMP = 0.1


def normalize_columns(balance):
    column_sum = lax.psum(jnp.sum(balance, axis=0), "batch")
    return balance / column_sum[None, :]


def crop_totals(balance):
    return lax.psum(jnp.sum(balance, axis=1), "proto")


def local(features, head_weight, student_scores):
    gathered = lax.all_gather(features, "proto", axis=0, tiled=True)
    feat_wide = gathered.astype(jnp.float32)
    fnorm = jnp.sqrt(jnp.sum(feat_wide * feat_wide, axis=1) + 1e-06)
    piece = lax.all_gather(head_weight, "batch", axis=0, tiled=True)
    piece_wide = piece.astype(jnp.float32)
    raw = jnp.dot(gathered, piece, preferred_element_type=jnp.float32)
    squares = jnp.sum(piece_wide * piece_wide, axis=0)
    wnorm = jnp.sqrt(squares + 1e-06)
    balance = jnp.exp(raw / (fnorm[:, None] * wnorm[None, :]) / TEACHER_TEMP)
    logits = student_scores.astype(jnp.float32) / STUDENT_TEMP
    exp_sums = jnp.sum(jnp.exp(logits), axis=2)
    for step in range(ITERS - 1):
        balance = normalize_columns(balance)
        balance = balance / crop_totals(balance)[:, None]
    balance = normalize_columns(balance)
    weighted = jnp.sum(logits * balance[None, :, :], axis=2)
    last_rows, total_exp, total_weighted = lax.psum(
        (jnp.sum(balance, axis=1), exp_sums, weighted), "proto"
    )
    balance = balance / last_rows[:, None]
    row_loss = jnp.log(total_exp) - total_weighted / last_rows[None, :]
    targets = (balance * PROTOS).astype(jnp.bfloat16)
    return (targets, row_loss)


def solution(mesh):
    return jax.shard_map(
        local,
        mesh=mesh,
        in_specs=(P(("batch", "proto"), None), P("batch", "proto"), P(None, "batch", "proto")),
        out_specs=(P("batch", "proto"), P(None, "batch")),
        check_vma=False,
    )
```

profile of v0, /device:TPU:0, one launch (start us, length us, event | category | flops | bytes accessed | tf_op | source)
XLA Modules:
  0.0 311.4 jit_solution(16653263350034114309)
XLA Ops:
  7.2 0.0 all-gather.2.cloned.1.call-start
  7.2 0.7 all-gather.2.cloned.1.call-update
  7.9 33.2 %all_gather.6 = bf16[1024,256]{1,0:T(8,128)(2,1)S(1)} all-gather(bf16[128,256]{1,0:T(8,128)(2,1)} %param.3), channel_id=1, replica_groups=mesh['batch'=4,'proto'=8] {'proto'}, dimensions={0}, use_global_device_ids=true | all-gather | bytes 589824 | tf_op jit(solution)/shard_map/all_gather | solution.py:22
  41.1 0.2 multiply_reduce_fusion.1
  41.4 5.4 %all-gather.2.cloned.1.call-done = bf16[256,8192]{1,0:T(8,128)(2,1)} async-done(((bf16[64,8192]{1,0:T(8,128)(2,1)}), bf16[256,8192]{1,0:T(8,128)(2,1)}) %all-gather.2.cloned.1.call-update) | async-done | bytes 4194320 | tf_op jit(solution)/shard_map/all_gather | solution.py:25
  46.7 3.1 multiply_reduce_fusion
  49.8 17.7 %fusion.16 = (f32[8192]{0:T(1024)S(1)}, f32[1024,8192]{1,0:T(8,128)}) fusion(f32[8192]{0:T(1024)S(1)} %add_sqrt_fusion, f32[1024]{0:T(1024)S(1)} %add_sqrt_fusion.1, bf16[1024,256]{1,0:T(8,128)(2,1)S(1)} %all_gather.6, bf16[256,8192]{1,0:T(8,128)(2,1)} %all-gather.2.cloned.1.call-done), kind=kOutput, calls=%fused_computation.28 | convolution fusion | flops 4328513536 | bytes 38342656 | tf_op jit(solution)/shard_map/dot_general | solution.py:27
  67.5 10.4 %psum.56 = f32[8192]{0:T(1024)S(1)} all-reduce(f32[8192]{0:T(1024)S(1)} %get-tuple-element.9), channel_id=1, replica_groups=mesh['batch'=4,'proto'=8] {'batch'}, use_global_device_ids=true, to_apply=%region_3.0 | all-reduce | flops 8192 | bytes 65536 | tf_op jit(solution)/shard_map/psum | solution.py:13
  77.9 12.2 %divide_reduce_fusion = f32[1024]{0:T(1024)S(1)} fusion(f32[1024,8192]{1,0:T(8,128)} %get-tuple-element.10, f32[8192]{0:T(1024)S(1)} %psum.56), kind=kLoop, calls=%fused_computation.16 | loop fusion | flops 16776192 | bytes 33591296 | tf_op jit(solution)/shard_map/reduce_sum | solution.py:18
  90.1 21.5 %psum.57 = f32[1024]{0:T(1024)S(1)} all-reduce(f32[1024]{0:T(1024)S(1)} %divide_reduce_fusion), channel_id=1, replica_groups=mesh['batch'=4,'proto'=8] {'proto'}, use_global_device_ids=true, to_apply=%region_5.0 | all-reduce | flops 1024 | bytes 8192 | tf_op jit(solution)/shard_map/psum | solution.py:18
  111.6 14.1 %fusion.11 = f32[8192]{0:T(1024)S(1)} fusion(f32[1024,8192]{1,0:T(8,128)} %get-tuple-element.10, f32[1024]{0:T(1024)S(1)} %psum.57, f32[8192]{0:T(1024)S(1)} %psum.56), kind=kLoop, calls=%fused_computation.17 | loop fusion | flops 25157632 | bytes 33624064 | tf_op jit(solution)/shard_map/reduce_sum | solution.py:13
  125.7 10.3 %psum.58 = f32[8192]{0:T(1024)S(1)} all-reduce(f32[8192]{0:T(1024)S(1)} %fusion.11), channel_id=1, replica_groups=mesh['batch'=4,'proto'=8] {'batch'}, use_global_device_ids=true, to_apply=%region_7.0 | all-reduce | flops 8192 | bytes 65536 | tf_op jit(solution)/shard_map/psum | solution.py:13
  136.0 14.1 %fusion.13 = f32[1024]{0:T(1024)S(1)} fusion(f32[1024,8192]{1,0:T(8,128)} %get-tuple-element.10, f32[8192]{0:T(1024)S(1)} %psum.58, f32[1024]{0:T(1024)S(1)} %psum.57, f32[8192]{0:T(1024)S(1)} %psum.56), kind=kLoop, calls=%fused_computation.19 | loop fusion | flops 33553408 | bytes 33628160 | tf_op jit(solution)/shard_map/reduce_sum | solution.py:18
  150.1 17.1 %psum.59 = f32[1024]{0:T(1024)S(1)} all-reduce(f32[1024]{0:T(1024)S(1)} %fusion.13), channel_id=1, replica_groups=mesh['batch'=4,'proto'=8] {'proto'}, use_global_device_ids=true, to_apply=%region_9.0 | all-reduce | flops 1024 | bytes 8192 | tf_op jit(solution)/shard_map/psum | solution.py:18
  167.3 14.5 %fusion.14 = f32[8192]{0:T(1024)S(1)} fusion(f32[1024,8192]{1,0:T(8,128)} %get-tuple-element.10, f32[1024]{0:T(1024)S(1)} %psum.59, f32[8192]{0:T(1024)S(1)} %psum.58, f32[1024]{0:T(1024)S(1)} %psum.57, f32[8192]{0:T(1024)S(1)} %psum.56), kind=kLoop, calls=%fused_computation.20 | loop fusion | flops 41934848 | bytes 33660928 | tf_op jit(solution)/shard_map/reduce_sum | solution.py:13
  181.7 10.4 %psum.60 = f32[8192]{0:T(1024)S(1)} all-reduce(f32[8192]{0:T(1024)S(1)} %fusion.14), channel_id=1, replica_groups=mesh['batch'=4,'proto'=8] {'batch'}, use_global_device_ids=true, to_apply=%region_11.0 | all-reduce | flops 8192 | bytes 65536 | tf_op jit(solution)/shard_map/psum | solution.py:13
  192.2 28.0 %broadcast_multiply_fusion = (f32[1024,8192]{1,0:T(8,128)}, f32[1024]{0:T(1024)S(1)}) fusion(f32[1024,8192]{1,0:T(8,128)} %get-tuple-element.10, f32[8192]{0:T(1024)S(1)} %psum.60, f32[1024]{0:T(1024)S(1)} %psum.59, f32[8192]{0:T(1024)S(1)} %psum.58, f32[1024]{0:T(1024)S(1)} %psum.57, f32[8192]{0:T(1024)S(1)} %psum.56), kind=kLoop, calls=%fused_computation.21 | loop fusion | flops 58719232 | bytes 67219456 | tf_op jit(solution)/shard_map/mul | solution.py:37
  220.2 27.8 %fusion.1 = (f32[2,1024]{1,0:T(2,128)S(1)}, f32[2,1024]{1,0:T(2,128)S(1)}) fusion(bf16[2,1024,8192]{2,1,0:T(8,128)(2,1)} %param.5, f32[1024,8192]{1,0:T(8,128)} %get-tuple-element.7), kind=kLoop, calls=%fused_computation.3 | loop fusion | flops 83881984 | bytes 67125248 | tf_op jit(solution)/shard_map/reduce_sum | solution.py:32
  248.0 34.9 %all-reduce = (f32[1024]{0:T(1024)S(1)}, f32[2,1024]{1,0:T(2,128)S(1)}, f32[2,1024]{1,0:T(2,128)S(1)}) all-reduce(f32[1024]{0:T(1024)S(1)} %get-tuple-element.8, f32[2,1024]{1,0:T(2,128)S(1)} %get-tuple-element.3, f32[2,1024]{1,0:T(2,128)S(1)} %get-tuple-element.2), channel_id=1, replica_groups=mesh['batch'=4,'proto'=8] {'proto'}, use_global_device_ids=true, to_apply=%region_13.0 | all-reduce | flops 5120 | bytes 40960 | tf_op jit(solution)/shard_map/psum | solution.py:38
  282.9 21.1 %fusion.12 = bf16[1024,8192]{1,0:T(8,128)(2,1)} fusion(f32[1024,8192]{1,0:T(8,128)} %get-tuple-element.10, f32[1024]{0:T(1024)S(1)} %get-tuple-element.4, f32[8192]{0:T(1024)S(1)} %psum.60, f32[1024]{0:T(1024)S(1)} %psum.59, f32[8192]{0:T(1024)S(1)} %psum.58, f32[1024]{0:T(1024)S(1)} %psum.57, f32[8192]{0:T(1024)S(1)} %psum.56), kind=kLoop, calls=%fused_computation.18 | loop fusion | flops 67108864 | bytes 50442240 | tf_op jit(solution)/shard_map/convert_element_type | solution.py:43
  303.9 0.6 divide_subtract_fusion
  (2 shorter events, 0.0 us)
Async XLA Ops:
  7.2 39.6 %all-gather.2.cloned.1.call-start = ((), (), s32[]{:S(2)}) async-start(), calls=%async_computation | async-start | bytes 5242880 | tf_op jit(solution)/shard_map/all_gather | solution.py:25
Sparse Core Ops, SparseCore 0:
  9.5 37.1 all-gather.1
where the time goes:
time: 312 us; the launch traced here: 311 us
  blocking collectives  138 us (44%)
  other arithmetic  136 us (44%)
  matrix products  17.7 us (6%)
  between operations  14.1 us (5%)
  waiting for transfers between devices  6.05 us (2%)
    psum x2, blocking collectives, crop_totals(): return lax.psum(jnp.sum(balance, axis=1), 'proto')  38.7 us
    psum x1, blocking collectives, local(): lax.psum((jnp.sum(balance, axis=1), exp_sums, weighted), 'proto')  34.9 us
    all_gather x1, blocking collectives, local(): gathered = lax.all_gather(features, 'proto', axis=0, tiled=True)  33.2 us
    psum x3, blocking collectives, normalize_columns(): column_sum = lax.psum(jnp.sum(balance, axis=0), 'batch')  31.1 us
    reduce_sum x2, other arithmetic, normalize_columns(): column_sum = lax.psum(jnp.sum(balance, axis=0), 'batch')  28.5 us
    mul x1, other arithmetic, local(): weighted = jnp.sum(logits * balance[None, :, :], axis=2)  28 us
    reduce_sum x1, other arithmetic, local(): exp_sums = jnp.sum(jnp.exp(logits), axis=2)  27.8 us
    reduce_sum x2, other arithmetic, crop_totals(): return lax.psum(jnp.sum(balance, axis=1), 'proto')  26.3 us
  transfers between devices with their start and end apart: 1, of which 1 were waited for; matrix products, arithmetic and copies ran while one was open for 0% of the time, Pallas kernels for 0%

commit v1 on v0

--- a/solution.py
+++ b/solution.py
@@ -7,6 +7,23 @@
 ITERS = 3
 TEACHER_TEMP = 0.07
 STUDENT_TEMP = 0.1
+
+
+def in_order(blocks, dim):
+    blocks = jnp.moveaxis(blocks, 0, dim)
+    dims = blocks.shape
+    return blocks.reshape(*dims[:dim], dims[dim] * dims[dim + 1], *dims[dim + 2 :])
+
+
+def doubled(x, axis):
+    size, index = (lax.axis_size(axis), lax.axis_index(axis))
+    parts, bit = (x[None], 1)
+    while bit < size:
+        other = lax.ppermute(parts, axis, [(i, i ^ bit) for i in range(size)])
+        low = index & bit == 0
+        parts = jnp.concatenate([jnp.where(low, parts, other), jnp.where(low, other, parts)])
+        bit *= 2
+    return parts
 
 
 def normalize_columns(balance):
@@ -19,7 +36,7 @@
 
 
 def local(features, head_weight, student_scores):
-    gathered = lax.all_gather(features, "proto", axis=0, tiled=True)
+    gathered = in_order(doubled(features, "proto"), 0)
     feat_wide = gathered.astype(jnp.float32)
     fnorm = jnp.sqrt(jnp.sum(feat_wide * feat_wide, axis=1) + 1e-06)
     piece = lax.all_gather(head_weight, "batch", axis=0, tiled=True)

time: 312 us -> 312 us (level)
  blocking collectives: 138 us -> 105 us
  waiting for transfers between devices: 6.05 us -> 30 us
  starting transfers between devices: 0.04 us -> 8.34 us
    all_gather x1 -> x0, blocking collectives: 33.2 us -> none  [local(): gathered = lax.all_gather(features, 'proto', axis=0, tiled=True)]
    ppermute x0 -> x3, waiting for transfers between devices: none -> 15 us  [doubled(): other = lax.ppermute(parts, axis, [(i, i ^ bit) for i in range(size)])]
    all_gather x1, waiting for transfers between devices: 5.37 us -> 14.2 us  [local(): piece = lax.all_gather(head_weight, 'batch', axis=0, tiled=True)]
    ppermute x0 -> x3, starting transfers between devices: none -> 8.3 us  [doubled(): other = lax.ppermute(parts, axis, [(i, i ^ bit) for i in range(size)])]
  transfers between devices with their start and end apart: 1 -> 4, of which waited for: 1 -> 4; matrix products, arithmetic and copies ran while one was open for 0% -> 0% of each run, Pallas kernels for 0% -> 0%
where the time goes in v1:
time: 312 us; the launch traced here: 311 us
  other arithmetic  137 us (44%)
  blocking collectives  105 us (34%)
  waiting for transfers between devices  30 us (10%)
  matrix products  17.7 us (6%)
  between operations  14.1 us (5%)
  starting transfers between devices  8.34 us (3%)
    psum x2, blocking collectives, crop_totals(): return lax.psum(jnp.sum(balance, axis=1), 'proto')  38.7 us
    psum x1, blocking collectives, local(): lax.psum((jnp.sum(balance, axis=1), exp_sums, weighted), 'proto')  34.9 us
    psum x3, blocking collectives, normalize_columns(): column_sum = lax.psum(jnp.sum(balance, axis=0), 'batch')  31.1 us
    reduce_sum x2, other arithmetic, normalize_columns(): column_sum = lax.psum(jnp.sum(balance, axis=0), 'batch')  28.5 us
    mul x1, other arithmetic, local(): weighted = jnp.sum(logits * balance[None, :, :], axis=2)  28 us
    reduce_sum x1, other arithmetic, local(): exp_sums = jnp.sum(jnp.exp(logits), axis=2)  27.8 us
    reduce_sum x2, other arithmetic, crop_totals(): return lax.psum(jnp.sum(balance, axis=1), 'proto')  26.3 us
    convert_element_type x1, other arithmetic, local(): targets = (balance * PROTOS).astype(jnp.bfloat16)  21.1 us
  transfers between devices with their start and end apart: 4, of which 4 were waited for; matrix products, arithmetic and copies ran while one was open for 0% of the time, Pallas kernels for 0%

profile of v1, /device:TPU:0, one launch (start us, length us, event | category | flops | bytes accessed | tf_op | source)
XLA Modules:
  0.0 311.4 jit_solution(16682762255544478980)
XLA Ops:
  7.2 0.0 all-gather.2.cloned.1.call-start
  7.2 0.7 all-gather.2.cloned.1.call-update
  7.9 3.0 collective-permute-start
  10.9 2.5 collective-permute-done
  13.4 0.9 broadcast_select_fusion.5
  14.3 2.2 collective-permute-start.1
  16.4 2.9 collective-permute-done.1
  19.4 3.1 collective-permute-start.2
  22.5 9.6 %collective-permute-done.2 = bf16[4,128,256]{2,1,0:T(8,128)(2,1)S(1)} collective-permute-done((bf16[4,128,256]{2,1,0:T(8,128)(2,1)S(1)}, bf16[4,128,256]{2,1,0:T(8,128)(2,1)S(1)}, u32[]{:S(2)}, u32[]{:S(2)}) %collective-permute-start.2) | collective-permute-done | bytes 262176 | tf_op jit(solution)/shard_map/ppermute | solution.py:22
  32.2 0.2 multiply_reduce_fusion.1
  32.5 14.2 %all-gather.2.cloned.1.call-done = bf16[256,8192]{1,0:T(8,128)(2,1)} async-done(((bf16[64,8192]{1,0:T(8,128)(2,1)}), bf16[256,8192]{1,0:T(8,128)(2,1)}) %all-gather.2.cloned.1.call-update) | async-done | bytes 4194320 | tf_op jit(solution)/shard_map/all_gather | solution.py:42
  46.7 3.1 multiply_reduce_fusion
  49.8 17.7 %fusion.16 = (f32[8192]{0:T(1024)S(1)}, f32[1024,8192]{1,0:T(8,128)}) fusion(f32[8192]{0:T(1024)S(1)} %add_sqrt_fusion, f32[1024]{0:T(1024)S(1)} %sqrt_bitcast_fusion, bf16[1024,256]{1,0:T(8,128)(2,1)S(1)} %bitcast.8, bf16[256,8192]{1,0:T(8,128)(2,1)} %all-gather.2.cloned.1.call-done), kind=kOutput, calls=%fused_computation.37 | convolution fusion | flops 4328513536 | bytes 38342656 | tf_op jit(solution)/shard_map/dot_general | solution.py:44
  67.5 10.4 %psum.56 = f32[8192]{0:T(1024)S(1)} all-reduce(f32[8192]{0:T(1024)S(1)} %get-tuple-element.15), channel_id=1, replica_groups=mesh['batch'=4,'proto'=8] {'batch'}, use_global_device_ids=true, to_apply=%region_3.4 | all-reduce | flops 8192 | bytes 65536 | tf_op jit(solution)/shard_map/psum | solution.py:30
  77.9 12.2 %divide_reduce_fusion = f32[1024]{0:T(1024)S(1)} fusion(f32[1024,8192]{1,0:T(8,128)} %get-tuple-element.16, f32[8192]{0:T(1024)S(1)} %psum.56), kind=kLoop, calls=%fused_computation.16 | loop fusion | flops 16776192 | bytes 33591296 | tf_op jit(solution)/shard_map/reduce_sum | solution.py:35
  90.1 21.5 %psum.57 = f32[1024]{0:T(1024)S(1)} all-reduce(f32[1024]{0:T(1024)S(1)} %divide_reduce_fusion), channel_id=1, replica_groups=mesh['batch'=4,'proto'=8] {'proto'}, use_global_device_ids=true, to_apply=%region_5.6 | all-reduce | flops 1024 | bytes 8192 | tf_op jit(solution)/shard_map/psum | solution.py:35
  111.6 14.1 %fusion.11 = f32[8192]{0:T(1024)S(1)} fusion(f32[1024,8192]{1,0:T(8,128)} %get-tuple-element.16, f32[1024]{0:T(1024)S(1)} %psum.57, f32[8192]{0:T(1024)S(1)} %psum.56), kind=kLoop, calls=%fused_computation.17 | loop fusion | flops 25157632 | bytes 33624064 | tf_op jit(solution)/shard_map/reduce_sum | solution.py:30
  125.7 10.3 %psum.58 = f32[8192]{0:T(1024)S(1)} all-reduce(f32[8192]{0:T(1024)S(1)} %fusion.11), channel_id=1, replica_groups=mesh['batch'=4,'proto'=8] {'batch'}, use_global_device_ids=true, to_apply=%region_7.8 | all-reduce | flops 8192 | bytes 65536 | tf_op jit(solution)/shard_map/psum | solution.py:30
  136.0 14.1 %fusion.13 = f32[1024]{0:T(1024)S(1)} fusion(f32[1024,8192]{1,0:T(8,128)} %get-tuple-element.16, f32[8192]{0:T(1024)S(1)} %psum.58, f32[1024]{0:T(1024)S(1)} %psum.57, f32[8192]{0:T(1024)S(1)} %psum.56), kind=kLoop, calls=%fused_computation.19 | loop fusion | flops 33553408 | bytes 33628160 | tf_op jit(solution)/shard_map/reduce_sum | solution.py:35
  150.1 17.1 %psum.59 = f32[1024]{0:T(1024)S(1)} all-reduce(f32[1024]{0:T(1024)S(1)} %fusion.13), channel_id=1, replica_groups=mesh['batch'=4,'proto'=8] {'proto'}, use_global_device_ids=true, to_apply=%region_9.10 | all-reduce | flops 1024 | bytes 8192 | tf_op jit(solution)/shard_map/psum | solution.py:35
  167.3 14.5 %fusion.14 = f32[8192]{0:T(1024)S(1)} fusion(f32[1024,8192]{1,0:T(8,128)} %get-tuple-element.16, f32[1024]{0:T(1024)S(1)} %psum.59, f32[8192]{0:T(1024)S(1)} %psum.58, f32[1024]{0:T(1024)S(1)} %psum.57, f32[8192]{0:T(1024)S(1)} %psum.56), kind=kLoop, calls=%fused_computation.20 | loop fusion | flops 41934848 | bytes 33660928 | tf_op jit(solution)/shard_map/reduce_sum | solution.py:30
  181.7 10.4 %psum.60 = f32[8192]{0:T(1024)S(1)} all-reduce(f32[8192]{0:T(1024)S(1)} %fusion.14), channel_id=1, replica_groups=mesh['batch'=4,'proto'=8] {'batch'}, use_global_device_ids=true, to_apply=%region_11.12 | all-reduce | flops 8192 | bytes 65536 | tf_op jit(solution)/shard_map/psum | solution.py:30
  192.2 28.0 %broadcast_multiply_fusion = (f32[1024,8192]{1,0:T(8,128)}, f32[1024]{0:T(1024)S(1)}) fusion(f32[1024,8192]{1,0:T(8,128)} %get-tuple-element.16, f32[8192]{0:T(1024)S(1)} %psum.60, f32[1024]{0:T(1024)S(1)} %psum.59, f32[8192]{0:T(1024)S(1)} %psum.58, f32[1024]{0:T(1024)S(1)} %psum.57, f32[8192]{0:T(1024)S(1)} %psum.56), kind=kLoop, calls=%fused_computation.21 | loop fusion | flops 58719232 | bytes 67219456 | tf_op jit(solution)/shard_map/mul | solution.py:54
  220.2 27.8 %fusion.1 = (f32[2,1024]{1,0:T(2,128)S(1)}, f32[2,1024]{1,0:T(2,128)S(1)}) fusion(bf16[2,1024,8192]{2,1,0:T(8,128)(2,1)} %param.5, f32[1024,8192]{1,0:T(8,128)} %get-tuple-element.7), kind=kLoop, calls=%fused_computation.3 | loop fusion | flops 83881984 | bytes 67125248 | tf_op jit(solution)/shard_map/reduce_sum | solution.py:49
  248.0 34.9 %all-reduce = (f32[1024]{0:T(1024)S(1)}, f32[2,1024]{1,0:T(2,128)S(1)}, f32[2,1024]{1,0:T(2,128)S(1)}) all-reduce(f32[1024]{0:T(1024)S(1)} %get-tuple-element.8, f32[2,1024]{1,0:T(2,128)S(1)} %get-tuple-element.3, f32[2,1024]{1,0:T(2,128)S(1)} %get-tuple-element.2), channel_id=1, replica_groups=mesh['batch'=4,'proto'=8] {'proto'}, use_global_device_ids=true, to_apply=%region_13.14 | all-reduce | flops 5120 | bytes 40960 | tf_op jit(solution)/shard_map/psum | solution.py:55
  282.9 21.1 %fusion.12 = bf16[1024,8192]{1,0:T(8,128)(2,1)} fusion(f32[1024,8192]{1,0:T(8,128)} %get-tuple-element.16, f32[1024]{0:T(1024)S(1)} %get-tuple-element.4, f32[8192]{0:T(1024)S(1)} %psum.60, f32[1024]{0:T(1024)S(1)} %psum.59, f32[8192]{0:T(1024)S(1)} %psum.58, f32[1024]{0:T(1024)S(1)} %psum.57, f32[8192]{0:T(1024)S(1)} %psum.56), kind=kLoop, calls=%fused_computation.18 | loop fusion | flops 67108864 | bytes 50442240 | tf_op jit(solution)/shard_map/convert_element_type | solution.py:60
  303.9 0.6 divide_subtract_fusion
  (7 shorter events, 0.2 us)
Async XLA Ops:
  7.2 39.6 %all-gather.2.cloned.1.call-start = ((), (), s32[]{:S(2)}) async-start(), calls=%async_computation | async-start | bytes 5242880 | tf_op jit(solution)/shard_map/all_gather | solution.py:42
  7.9 5.5 %collective-permute-start = (bf16[1,128,256]{2,1,0:T(8,128)(2,1)}, bf16[1,128,256]{2,1,0:T(8,128)(2,1)S(1)}, u32[]{:S(2)}, u32[]{:S(2)}) collective-permute-start(bf16[1,128,256]{2,1,0:T(8,128)(2,1)} %bitcast.9), channel_id=1, source_target_pairs={{0,1},{1,0},{2,3},{3,2},{4,5},{5,4},{6,7},{7,6},{8,9},{9,8},{10,11... | collective-permute-start | bytes 196616 | tf_op jit(solution)/shard_map/ppermute | solution.py:22
  14.3 5.1 %collective-permute-start.1 = (bf16[2,128,256]{2,1,0:T(8,128)(2,1)S(1)}, bf16[2,128,256]{2,1,0:T(8,128)(2,1)S(1)}, u32[]{:S(2)}, u32[]{:S(2)}) collective-permute-start(bf16[2,128,256]{2,1,0:T(8,128)(2,1)S(1)} %pad_maximum_fusion.2), channel_id=1, source_target_pairs={{0,2},{1,3},{2,0},{3,1},{4,6},{5,7},{6,4},{7,5},{8,10},{9,11},{10,... | collective-permute-start | bytes 393224 | tf_op jit(solution)/shard_map/ppermute | solution.py:22
  19.4 12.7 %collective-permute-start.2 = (bf16[4,128,256]{2,1,0:T(8,128)(2,1)S(1)}, bf16[4,128,256]{2,1,0:T(8,128)(2,1)S(1)}, u32[]{:S(2)}, u32[]{:S(2)}) collective-permute-start(bf16[4,128,256]{2,1,0:T(8,128)(2,1)S(1)} %pad_maximum_fusion.1), channel_id=1, source_target_pairs={{0,4},{1,5},{2,6},{3,7},{4,0},{5,1},{6,2},{7,3},{8,12},{9,13},{10,... | collective-permute-start | bytes 786440 | tf_op jit(solution)/shard_map/ppermute | solution.py:22
Sparse Core Ops, SparseCore 0:
  9.5 37.1 all-gather.1
